TPU v7x, 32 devices: a whole 2x2x4 slice. The times are simulated.
32 devices in a mesh: dp: 8 (over z, core), expert: 4 (over y, x).
Axes of the slice: x: 2, y: 2, z: 4, core: 2. Of those that a mesh axis runs over, the one named last changes fastest.
Arguments:
- tokens: bfloat16 [5120, 2048], P(('dp', 'expert')), may hold values from -6 to 6
- expert_ids: int32 [5120, 8], P(('dp', 'expert')), may hold values from 0 to 122, as said below
- gate_probs: float32 [5120, 8], P(('dp', 'expert')), may hold values from 0.02 to 1
- upstream: bfloat16 [5120, 2048], P(('dp', 'expert')), may hold values from -6 to 6
- w_gate: bfloat16 [4, 2048, 768], P('expert'), may hold values from -0.125 to 0.125
- w_up: bfloat16 [4, 2048, 768], P('expert'), may hold values from -0.125 to 0.125
- w_down: bfloat16 [4, 2048, 768], P('expert'), may hold values from -0.21875 to 0.21875
Outputs:
- layer_out: bfloat16 [5120, 2048], P(('dp', 'expert'))
- grad_tokens: bfloat16 [5120, 2048], P(('dp', 'expert'))
- grad_probs: float32 [5120, 8], P(('dp', 'expert'))
- grad_gate: float32 [4, 2048, 768], P('expert', 'dp')
- grad_up: float32 [4, 2048, 768], P('expert', 'dp')
- grad_down: float32 [4, 2048, 768], P('expert', 'dp')
Inputs may be any that keep to these rules, and one draw needn't show every extreme that they name: `expert_ids`: slot 0 of every token names one of the experts 0 to 3, the experts computed here; slot k, for k from 1 to 7, names an expert from 4 + (k - 1) * 17 to 4 + k * 17 - 1. `expert_ids`: among the 160 tokens of one device, slot 0 names no expert more than 100 times; on every index of dp one expert is named by slot 0 exactly 100 times by the tokens of each device of that index.
All inputs are finite; a program needn't handle non-finite values.
Results may differ from a plain program's by a relative error of at most 0.0058.
Values may be sent and summed in bfloat16 or wider, within the bound.
A program may use at most 128 MiB of HBM per device.

v0:
```python
import jax
import jax.numpy as jnp
from jax import lax
from jax.sharding import PartitionSpec as P


def times_transposed(left, right):
    return lax.dot_general(
        left, right, (((1,), (1,)), ((), ())), preferred_element_type=jnp.float32
    )


def contract_rows(left, right):
    return lax.dot_general(
        left, right, (((0,), (0,)), ((), ())), preferred_element_type=jnp.float32
    )


def expert_hidden(flat_rows, gate_mat, up_mat):
    pre_gate = jnp.dot(flat_rows, gate_mat, preferred_element_type=jnp.float32)
    pre_up = jnp.dot(flat_rows, up_mat, preferred_element_type=jnp.float32)
    hidden = (pre_gate * jax.nn.sigmoid(pre_gate) * pre_up).astype(jnp.bfloat16)
    return (hidden, pre_gate, pre_up)


def per_device(tokens, expert_ids, gate_probs, upstream, w_gate, w_up, w_down):
    tok_count, model_width = tokens.shape
    owners = lax.axis_size("expert")
    capacity = tok_count // owners * 5 // 2
    gate_mat = w_gate[0]
    up_mat = w_up[0]
    down_mat = w_down[0]
    hidden_width = gate_mat.shape[1]
    first_expert = expert_ids[:, 0]
    matches = (first_expert[:, None] == jnp.arange(owners, dtype=jnp.int32)[None, :]).astype(
        jnp.int32
    )
    earlier = jnp.cumsum(matches, axis=0) - matches
    target = first_expert * capacity + jnp.sum(earlier * matches, axis=1)

    def pack_rows(values):
        buffer = (
            jnp.zeros((owners * capacity, values.shape[1]), values.dtype).at[target].set(values)
        )
        return buffer.reshape(owners, capacity, values.shape[1])

    def unpack_rows(blocks):
        return blocks.reshape(owners * capacity, blocks.shape[2])[target]

    prob_total = jnp.sum(gate_probs, axis=1)
    gate_share = gate_probs[:, 0] / prob_total
    cotangent = (gate_share[:, None] * upstream.astype(jnp.float32)).astype(jnp.bfloat16)
    received = lax.all_to_all(pack_rows(tokens), "expert", split_axis=0, concat_axis=0, tiled=True)
    item_count = received.shape[1]
    forward_hidden, pre_gate, pre_up = expert_hidden(
        received.reshape(-1, model_width), gate_mat, up_mat
    )
    expert_out = times_transposed(forward_hidden, down_mat).astype(jnp.bfloat16)

    def split_items(values):
        return values.reshape(owners, item_count, values.shape[1])

    results = (
        split_items(expert_out),
        received,
        split_items(forward_hidden),
        split_items(pre_gate),
        split_items(pre_up),
    )
    arrived = results[1].reshape(-1, model_width)
    hidden = results[2].reshape(-1, hidden_width)
    pre_gate = results[3].reshape(-1, hidden_width)
    pre_up = results[4].reshape(-1, hidden_width)
    returned = lax.all_to_all(results[0], "expert", split_axis=0, concat_axis=0, tiled=True)
    mixed = unpack_rows(returned)
    layer_out = (gate_share[:, None] * mixed.astype(jnp.float32)).astype(jnp.bfloat16)
    gate_product = jnp.sum(upstream.astype(jnp.float32) * mixed.astype(jnp.float32), axis=1)
    first_slot = (jnp.arange(gate_probs.shape[1]) == 0).astype(jnp.float32)
    grad_probs = (first_slot[None, :] - gate_share[:, None]) * (gate_product / prob_total)[:, None]
    cot_arrived = lax.all_to_all(
        pack_rows(cotangent), "expert", split_axis=0, concat_axis=0, tiled=True
    ).reshape(-1, model_width)
    down_sum = lax.psum_scatter(
        contract_rows(cot_arrived, hidden), "dp", scatter_dimension=0, tiled=True
    )
    grad_hidden = jnp.dot(cot_arrived, down_mat, preferred_element_type=jnp.float32)
    sigmoid_gate = jax.nn.sigmoid(pre_gate)
    grad_pre_gate = (
        grad_hidden * pre_up * sigmoid_gate * (1.0 + pre_gate * (1.0 - sigmoid_gate))
    ).astype(jnp.bfloat16)
    grad_pre_up = (grad_hidden * pre_gate * sigmoid_gate).astype(jnp.bfloat16)
    both_grads = jnp.concatenate([grad_pre_gate, grad_pre_up], axis=1)
    input_sum = lax.psum_scatter(
        contract_rows(arrived, both_grads), "dp", scatter_dimension=0, tiled=True
    )
    gate_sum = input_sum[:, :hidden_width]
    up_sum = input_sum[:, hidden_width:]
    input_rows = (
        times_transposed(grad_pre_gate, gate_mat) + times_transposed(grad_pre_up, up_mat)
    ).astype(jnp.bfloat16)
    returned_grad = lax.all_to_all(
        input_rows.reshape(owners, capacity, model_width),
        "expert",
        split_axis=0,
        concat_axis=0,
        tiled=True,
    )
    grad_tokens = unpack_rows(returned_grad)
    return (layer_out, grad_tokens, grad_probs, gate_sum[None], up_sum[None], down_sum[None])


def solution(mesh):
    in_specs = (
        P(("dp", "expert"), None),
        P(("dp", "expert"), None),
        P(("dp", "expert"), None),
        P(("dp", "expert"), None),
        P("expert", None, None),
        P("expert", None, None),
        P("expert", None, None),
    )
    out_specs = (
        P(("dp", "expert"), None),
        P(("dp", "expert"), None),
        P(("dp", "expert"), None),
        P("expert", "dp", None),
        P("expert", "dp", None),
        P("expert", "dp", None),
    )
    return jax.shard_map(
        per_device, mesh=mesh, in_specs=in_specs, out_specs=out_specs, check_vma=False
    )
```

profile of v0, /device:TPU:0, one launch (start us, length us, event | category | flops | bytes accessed | tf_op | source)
XLA Modules:
  0.0 293.8 jit_solution(16600869608314591561)
XLA Ops:
  7.2 0.9 reduce_sum.31
  8.0 0.8 slice_divide_fusion
  8.8 0.7 slice.22
  9.6 1.2 reduce-window.6
  10.8 0.1 slice.32
  10.9 0.1 copy.15
  11.0 0.1 copy.16
  11.1 0.1 add_bitcast_fusion
  11.2 0.7 compare_select_fusion
  11.9 3.6 %scatter_custom_fusion.1 = bf16[400,2048]{1,0:T(8,128)(2,1)} fusion(s32[160]{0:T(256)S(1)} %bitcast.58, bf16[]{:T(256)} %constant.8.clone.1, bf16[160,2048]{1,0:T(8,128)(2,1)} %param.10, f32[160]{0:T(256)S(1)} %bitcast.51), kind=kCustom, calls=%fused_computation.32 | custom fusion | flops 983040 | bytes 2294786 | tf_op jit(solution)/shard_map/scatter | solution.py:43
  15.5 2.5 reshape.66
  18.0 5.2 %all-to-all-start.2 = ((bf16[4,100,2048]{2,1,0:T(8,128)(2,1)}), bf16[4,100,2048]{2,1,0:T(8,128)(2,1)}, u32[]{:S(2)}, u32[]{:S(2)}) async-start(bf16[4,100,2048]{2,1,0:T(8,128)(2,1)} %reshape.66), calls=%async_computation.2 | async-start | bytes 3407872 | tf_op jit(solution)/shard_map/all_to_all | solution.py:80
  23.2 3.5 %scatter_custom_fusion = bf16[400,2048]{1,0:T(8,128)(2,1)} fusion(s32[160]{0:T(256)S(1)} %bitcast.59, bf16[160,2048]{1,0:T(8,128)(2,1)} %param.7, bf16[]{:T(256)} %constant.8.clone.1), kind=kCustom, calls=%fused_computation.34 | custom fusion | bytes 1638912 | tf_op jit(solution)/shard_map/scatter | solution.py:43
  26.7 2.5 reshape.62
  29.2 15.4 %all-to-all-done.2 = bf16[4,100,2048]{2,1,0:T(8,128)(2,1)} async-done(((bf16[4,100,2048]{2,1,0:T(8,128)(2,1)}), bf16[4,100,2048]{2,1,0:T(8,128)(2,1)}, u32[]{:S(2)}, u32[]{:S(2)}) %all-to-all-start.2) | async-done | bytes 1638432 | tf_op jit(solution)/shard_map/all_to_all | solution.py:80
  44.6 4.4 %all-to-all-start = ((bf16[4,100,2048]{2,1,0:T(8,128)(2,1)}), bf16[4,100,2048]{2,1,0:T(8,128)(2,1)}, u32[]{:S(2)}, u32[]{:S(2)}) async-start(bf16[4,100,2048]{2,1,0:T(8,128)(2,1)} %reshape.62), calls=%async_computation | async-start | bytes 3407872 | tf_op jit(solution)/shard_map/all_to_all | solution.py:53
  49.0 0.0 reduce-scatter.3.cloned.1.call-start
  49.0 2.5 reshape.67
  51.6 4.9 %fusion = f32[400,768]{1,0:T(8,128)} fusion(bf16[400,2048]{1,0:T(8,128)(2,1)} %reshape.67, bf16[1,2048,768]{2,1,0:T(8,128)(2,1)} %param.13), kind=kOutput, calls=%fused_computation.5 | convolution fusion | flops 1258291200 | bytes 6012928 | tf_op jit(solution)/shard_map/dot_general | solution.py:86
  56.4 13.0 %all-to-all-done = bf16[4,100,2048]{2,1,0:T(8,128)(2,1)} async-done(((bf16[4,100,2048]{2,1,0:T(8,128)(2,1)}), bf16[4,100,2048]{2,1,0:T(8,128)(2,1)}, u32[]{:S(2)}, u32[]{:S(2)}) %all-to-all-start) | async-done | bytes 1638432 | tf_op jit(solution)/shard_map/all_to_all | solution.py:53
  69.4 2.5 reshape.63
  72.0 4.0 %fusion.6 = f32[400,768]{1,0:T(8,128)S(1)} fusion(bf16[400,2048]{1,0:T(8,128)(2,1)} %reshape.63, bf16[1,2048,768]{2,1,0:T(8,128)(2,1)} %param.12), kind=kOutput, calls=%fused_computation.11 | convolution fusion | flops 1258291200 | bytes 6012928 | tf_op jit(solution)/shard_map/dot_general | solution.py:21
  76.0 2.7 multiply_convert_fusion.1
  78.6 0.8 copy-done.2
  79.5 0.2 copy-done.4
  79.7 6.6 %fusion.20 = f32[2048,1536]{1,0:T(8,128)} fusion(bf16[400,2048]{1,0:T(8,128)(2,1)S(1)} %copy-done.1, bf16[400,768]{1,0:T(8,128)(2,1)S(1)} %get-tuple-element.8, bf16[400,768]{1,0:T(8,128)(2,1)S(1)} %get-tuple-element.6), kind=kOutput, calls=%fused_computation.24 | convolution fusion | flops 2519040000 | bytes 15450112 | tf_op jit(solution)/shard_map/dot_general | solution.py:14
  86.2 0.0 reduce-scatter.3.cloned.1.call-update
  86.3 0.2 reduce-scatter.5.cloned.1.call-start
  86.5 6.0 %fusion.33 = f32[2048,768]{1,0:T(8,128)} fusion(bf16[400,2048]{1,0:T(8,128)(2,1)} %reshape.67, bf16[400,768]{1,0:T(8,128)(2,1)} %get-tuple-element.7), kind=kOutput, calls=%fused_computation.53 | convolution fusion | flops 1258291200 | bytes 8544256 | tf_op jit(solution)/shard_map/dot_general | solution.py:14
  92.5 0.0 reduce-scatter.5.cloned.1.call-update
  92.5 5.3 %fusion.12 = bf16[400,2048]{1,0:T(8,128)(2,1)} fusion(bf16[400,768]{1,0:T(8,128)(2,1)} %get-tuple-element.7, bf16[1,2048,768]{2,1,0:T(8,128)(2,1)} %param.13), kind=kOutput, calls=%fused_computation.17 | convolution fusion | flops 1259110400 | bytes 5398528 | tf_op jit(solution)/shard_map/dot_general | solution.py:8
  97.9 2.5 reshape.64
  100.4 4.4 %all-to-all-start.1 = ((bf16[4,100,2048]{2,1,0:T(8,128)(2,1)}), bf16[4,100,2048]{2,1,0:T(8,128)(2,1)}, u32[]{:S(2)}, u32[]{:S(2)}) async-start(bf16[4,100,2048]{2,1,0:T(8,128)(2,1)} %reshape.64), calls=%async_computation.1 | async-start | bytes 3407872 | tf_op jit(solution)/shard_map/all_to_all | solution.py:74
  104.8 3.7 %fusion.4 = f32[400,2048]{1,0:T(8,128)S(1)} fusion(bf16[400,768]{1,0:T(8,128)(2,1)} %copy-done.2, bf16[1,2048,768]{2,1,0:T(8,128)(2,1)} %param.12), kind=kOutput, calls=%fused_computation.9 | convolution fusion | flops 1258291200 | bytes 7036928 | tf_op jit(solution)/shard_map/dot_general | solution.py:8
  108.5 2.7 add_convert_fusion
  111.2 2.5 reshape.68
  113.7 11.3 %all-to-all-done.1 = bf16[4,100,2048]{2,1,0:T(8,128)(2,1)} async-done(((bf16[4,100,2048]{2,1,0:T(8,128)(2,1)}), bf16[4,100,2048]{2,1,0:T(8,128)(2,1)}, u32[]{:S(2)}, u32[]{:S(2)}) %all-to-all-start.1) | async-done | bytes 1638432 | tf_op jit(solution)/shard_map/all_to_all | solution.py:74
  125.0 4.4 %all-to-all-start.3 = ((bf16[4,100,2048]{2,1,0:T(8,128)(2,1)}), bf16[4,100,2048]{2,1,0:T(8,128)(2,1)}, u32[]{:S(2)}, u32[]{:S(2)}) async-start(bf16[4,100,2048]{2,1,0:T(8,128)(2,1)} %reshape.68), calls=%async_computation.3 | async-start | bytes 3407872 | tf_op jit(solution)/shard_map/all_to_all | solution.py:101
  129.5 2.6 reshape.65
  132.1 4.2 %gather_fusion = bf16[160,2048]{1,0:T(8,128)(2,1)} fusion(bf16[400,2048]{1,0:T(8,128)(2,1)} %reshape.65, s32[1024]{0:T(1024)S(1)} %pad_clamp_fusion), kind=kCustom, calls=%fused_computation | custom fusion | bytes 1311360 | tf_op jit(solution)/shard_map/gather | solution.py:48
  136.2 2.5 fusion.19
  138.7 10.9 %all-to-all-done.3 = bf16[4,100,2048]{2,1,0:T(8,128)(2,1)} async-done(((bf16[4,100,2048]{2,1,0:T(8,128)(2,1)}), bf16[4,100,2048]{2,1,0:T(8,128)(2,1)}, u32[]{:S(2)}, u32[]{:S(2)}) %all-to-all-start.3) | async-done | bytes 1638432 | tf_op jit(solution)/shard_map/all_to_all | solution.py:101
  149.6 2.5 reshape.69
  152.1 4.2 %gather_fusion.1 = bf16[160,2048]{1,0:T(8,128)(2,1)} fusion(bf16[400,2048]{1,0:T(8,128)(2,1)} %reshape.69, s32[1024]{0:T(1024)S(1)} %pad_clamp_fusion), kind=kCustom, calls=%fused_computation.1 | custom fusion | bytes 1311360 | tf_op jit(solution)/shard_map/gather | solution.py:48
  156.3 0.7 subtract_multiply_fusion
  157.0 58.9 %reduce-scatter.3.cloned.1.call-done = f32[256,1536]{1,0:T(8,128)} async-done(((f32[2048,1536]{1,0:T(8,128)}), f32[256,1536]{1,0:T(8,128)}) %reduce-scatter.3.cloned.1.call-update) | async-done | bytes 1572880 | tf_op jit(solution)/shard_map/reduce_scatter | solution.py:93
  215.9 2.6 slice_bitcast_fusion
  218.5 68.4 %reduce-scatter.5.cloned.1.call-done = f32[256,768]{1,0:T(8,128)} async-done(((f32[2048,768]{1,0:T(8,128)}), f32[256,768]{1,0:T(8,128)}) %reduce-scatter.5.cloned.1.call-update) | async-done | bytes 786448 | tf_op jit(solution)/shard_map/reduce_scatter | solution.py:83
  (20 shorter events, 0.1 us)
Async XLA Ops:
  7.2 68.8 %copy-start = (bf16[1,2048,768]{2,1,0:T(8,128)(2,1)S(1)}, bf16[1,2048,768]{2,1,0:T(8,128)(2,1)}, u32[]{:S(2)}) copy-start(bf16[1,2048,768]{2,1,0:T(8,128)(2,1)} %param.11) | copy-start | bytes 9437188
  18.0 26.6 %all-to-all-start.2 = ((bf16[4,100,2048]{2,1,0:T(8,128)(2,1)}), bf16[4,100,2048]{2,1,0:T(8,128)(2,1)}, u32[]{:S(2)}, u32[]{:S(2)}) async-start(bf16[4,100,2048]{2,1,0:T(8,128)(2,1)} %reshape.66), calls=%async_computation.2 | async-start | bytes 3407872 | tf_op jit(solution)/shard_map/all_to_all | solution.py:80
  44.6 24.8 %all-to-all-start = ((bf16[4,100,2048]{2,1,0:T(8,128)(2,1)}), bf16[4,100,2048]{2,1,0:T(8,128)(2,1)}, u32[]{:S(2)}, u32[]{:S(2)}) async-start(bf16[4,100,2048]{2,1,0:T(8,128)(2,1)} %reshape.62), calls=%async_computation | async-start | bytes 3407872 | tf_op jit(solution)/shard_map/all_to_all | solution.py:53
  49.0 166.9 %reduce-scatter.3.cloned.1.call-start = ((), (), s32[]{:S(2)}) async-start(), calls=%async_computation.6 | async-start | bytes 14155776 | tf_op jit(solution)/shard_map/reduce_scatter | solution.py:93
  72.0 4.0 %copy-start.1 = (bf16[400,2048]{1,0:T(8,128)(2,1)S(1)}, bf16[400,2048]{1,0:T(8,128)(2,1)}, u32[]{:S(2)}) copy-start(bf16[400,2048]{1,0:T(8,128)(2,1)} %reshape.63) | copy-start | bytes 4915204
  72.0 4.0 %copy-start.3 = (f32[400,768]{1,0:T(8,128)S(1)}, f32[400,768]{1,0:T(8,128)}, u32[]{:S(2)}) copy-start(f32[400,768]{1,0:T(8,128)} %fusion) | copy-start | bytes 3686404
  78.6 0.8 copy-start.2
  78.6 1.0 copy-start.4
  86.3 200.7 %reduce-scatter.5.cloned.1.call-start = ((), (), s32[]{:S(2)}) async-start(), calls=%async_computation.7 | async-start | bytes 7077888 | tf_op jit(solution)/shard_map/reduce_scatter | solution.py:83
  100.4 24.6 %all-to-all-start.1 = ((bf16[4,100,2048]{2,1,0:T(8,128)(2,1)}), bf16[4,100,2048]{2,1,0:T(8,128)(2,1)}, u32[]{:S(2)}, u32[]{:S(2)}) async-start(bf16[4,100,2048]{2,1,0:T(8,128)(2,1)} %reshape.64), calls=%async_computation.1 | async-start | bytes 3407872 | tf_op jit(solution)/shard_map/all_to_all | solution.py:74
  104.8 3.7 %copy-start.5 = (bf16[400,768]{1,0:T(8,128)(2,1)S(1)}, bf16[400,768]{1,0:T(8,128)(2,1)}, u32[]{:S(2)}) copy-start(bf16[400,768]{1,0:T(8,128)(2,1)} %copy-done.4) | copy-start | bytes 1843204
  125.0 24.6 %all-to-all-start.3 = ((bf16[4,100,2048]{2,1,0:T(8,128)(2,1)}), bf16[4,100,2048]{2,1,0:T(8,128)(2,1)}, u32[]{:S(2)}, u32[]{:S(2)}) async-start(bf16[4,100,2048]{2,1,0:T(8,128)(2,1)} %reshape.68), calls=%async_computation.3 | async-start | bytes 3407872 | tf_op jit(solution)/shard_map/all_to_all | solution.py:101
Sparse Core Ops, SparseCore 0:
  86.4 129.5 reduce-scatter.2
  218.8 68.1 reduce-scatter.4
where the time goes:
time: 295 us; the launch traced here: 294 us
  waiting for transfers between devices  178 us (60%)
  local copies, waits for them, and re-layouts  36.7 us (12%)
  matrix products  35.9 us (12%)
  starting transfers between devices  18.6 us (6%)
  between operations  14.2 us (5%)
  other arithmetic  10.4 us (4%)
    reduce_scatter x1, waiting for transfers between devices, per_device(): lax.psum_scatter(contract_rows(cot_arrived, hidden), 'dp', scatter_dimens...  68.4 us
    reduce_scatter x1, waiting for transfers between devices, per_device(): lax.psum_scatter(contract_rows(arrived, both_grads), 'dp', scatter_dimens...  58.9 us
    all_to_all x1, waiting for transfers between devices, per_device(): lax.all_to_all(pack_rows(cotangent), 'expert', split_axis=0, concat_axis=...  15.4 us
    all_to_all x1, waiting for transfers between devices, per_device(): lax.all_to_all(pack_rows(tokens), 'expert', split_axis=0, concat_axis=0,...  13 us
    dot_general x2, matrix products, contract_rows(): lax.dot_general(left, right, (((0,), (0,)), ((), ())), preferred_element_...  12.6 us
    dot_general x3, matrix products, times_transposed(): lax.dot_general(left, right, (((1,), (1,)), ((), ())), preferred_element_...  11.8 us
    all_to_all x1, waiting for transfers between devices, per_device(): lax.all_to_all(results[0], 'expert', split_axis=0, concat_axis=0, tiled=T...  11.3 us
    all_to_all x1, waiting for transfers between devices, per_device(): lax.all_to_all(input_rows.reshape(owners, capacity, model_width), 'expert...  10.9 us
  transfers between devices with their start and end apart: 6, of which 6 were waited for; matrix products, arithmetic and copies ran while one was open for 19% of the time, Pallas kernels for 0%

commit v1 on v0

v1 whole, which is shorter than its diff:
```python
import functools

import jax
import jax.numpy as jnp
from jax import lax
from jax.experimental import pallas as pl
from jax.experimental.pallas import tpu as pltpu
from jax.sharding import PartitionSpec as P

MESH = pl.DeviceIdType.MESH
F32 = jnp.float32
BF16 = jnp.bfloat16


def dot_nn(a, b):
    return lax.dot_general(a, b, (((1,), (0,)), ((), ())), preferred_element_type=F32)


def dot_nt(a, b):
    return lax.dot_general(a, b, (((1,), (1,)), ((), ())), preferred_element_type=F32)


def dot_tn(a, b):
    return lax.dot_general(a, b, (((0,), (0,)), ((), ())), preferred_element_type=F32)


def loop(count, body):
    def step(i, carry):
        body(i)
        return carry

    lax.fori_loop(0, count, step, 0)


def moe_kernel(
    owners, copies, cap,
    ids_ref, probs_ref, tok_ref, ups_ref, wg_hbm, wu_hbm, wd_hbm,
    out_ref, gtok_ref, gprob_ref, ggate_ref, gup_ref, gdown_ref,
    wg, wu, wd, onehot, xs, cs, xr, cr, ors, grs, pre_g, pre_u, hid, gpg, gpu,
    sib_s, sib_r, z_s, z_l, z_r, tmp,
    w_sem, x_ss, x_rs, c_ss, c_rs, o_ss, o_rs, g_ss, g_rs,
    sib_ss, sib_rs, z_ss, z_ls, z_rs,
):
    me = lax.axis_index("expert")
    dp = lax.axis_index("dp")
    levels = copies // 2
    core = lax.rem(dp, 2)
    z = dp // 2
    tok_count, width = tok_ref.shape
    ff = hid.shape[1]
    rows = width // copies
    ft = 256
    dt = 256
    sibling = {"dp": dp + 1 - 2 * core}
    right = {"dp": lax.rem(dp + 2, copies)}
    left = {"dp": lax.rem(dp + copies - 2, copies)}

    w_copies = [
        pltpu.make_async_copy(src.at[0], dst, w_sem.at[i])
        for i, (src, dst) in enumerate(((wg_hbm, wg), (wu_hbm, wu), (wd_hbm, wd)))
    ]
    for copy in w_copies:
        copy.start()

    barrier = pltpu.get_barrier_semaphore()

    def greet(k):
        pl.semaphore_signal(
            barrier, inc=1, device_id={"expert": lax.rem(me + k + 1, owners)}, device_id_type=MESH
        )

    loop(owners - 1, greet)
    pl.semaphore_signal(barrier, inc=1, device_id=sibling, device_id_type=MESH)

    @pl.when(z > 0)
    def _():
        pl.semaphore_signal(barrier, inc=1, device_id=left, device_id_type=MESH)

    @pl.when(z < levels - 1)
    def _():
        pl.semaphore_signal(barrier, inc=1, device_id=right, device_id_type=MESH)

    ids = ids_ref[...]
    experts = lax.broadcasted_iota(jnp.int32, (max(owners, 8), tok_count), 0)
    match = (experts == ids).astype(BF16)
    before = (
        lax.broadcasted_iota(jnp.int32, (tok_count, tok_count), 0)
        < lax.broadcasted_iota(jnp.int32, (tok_count, tok_count), 1)
    ).astype(BF16)
    rank = jnp.sum(dot_nn(match, before) * match.astype(F32), axis=0, keepdims=True)
    target = ids * cap + rank.astype(jnp.int32)
    slots = lax.broadcasted_iota(jnp.int32, (owners * cap, tok_count), 0)
    onehot[...] = (slots == target).astype(BF16)

    probs = probs_ref[...]
    total = jnp.sum(probs, axis=1, keepdims=True)
    share = probs[:, 0:1] / total

    def block(index):
        return pl.ds(pl.multiple_of(index * cap, 8), cap)

    def exchange(src, dst, ss, rs, k):
        peer = lax.rem(me + k + 1, owners)
        return pltpu.make_async_remote_copy(
            src_ref=src.at[block(peer)],
            dst_ref=dst.at[block(me)],
            send_sem=ss.at[k],
            recv_sem=rs.at[k],
            device_id={"expert": peer},
            device_id_type=MESH,
        )

    beside = (z + levels - 1) // levels + (2 * levels - 2 - z) // levels
    pl.semaphore_wait(barrier, owners + beside)

    def dispatch(values, src, dst, ss, rs):
        def one(k):
            peer = lax.rem(me + k + 1, owners)
            src[block(peer)] = dot_nn(onehot[block(peer)], values[...]).astype(BF16)
            exchange(src, dst, ss, rs, k).start()

        loop(owners - 1, one)
        dst[block(me)] = dot_nn(onehot[block(me)], values[...]).astype(BF16)

    dispatch(tok_ref, xs, xr, x_ss, x_rs)
    gtok_ref[...] = (share * ups_ref[...].astype(F32)).astype(BF16)
    dispatch(gtok_ref, cs, cr, c_ss, c_rs)

    w_copies[0].wait()
    w_copies[1].wait()
    loop(owners - 1, lambda k: exchange(xs, xr, x_ss, x_rs, k).wait_recv())

    def forward_tile(j):
        cols = pl.ds(pl.multiple_of(j * ft, 128), ft)
        a = dot_nn(xr[...], wg[:, cols])
        b = dot_nn(xr[...], wu[:, cols])
        pre_g[:, cols] = a
        pre_u[:, cols] = b
        hid[:, cols] = (a * jax.nn.sigmoid(a) * b).astype(BF16)

    loop(ff // ft, forward_tile)

    w_copies[2].wait()
    loop(owners - 1, lambda k: exchange(xs, xr, x_ss, x_rs, k).wait_send())

    def out_tile(j):
        cols = pl.ds(pl.multiple_of(j * dt, 128), dt)
        xs[:, cols] = dot_nt(hid[...], wd[cols, :]).astype(BF16)

    loop(width // dt, out_tile)
    ors[block(me)] = xs[block(me)]

    loop(owners - 1, lambda k: exchange(cs, cr, c_ss, c_rs, k).wait_recv())

    sides = ((cr, hid), (xr, gpg), (xr, gpu))

    def piece(m, dest):
        lhs, rhs = sides[m]
        cols = pl.ds(pl.multiple_of(dest * rows, 128), rows)
        return dot_tn(lhs[:, cols], rhs[...])

    def sib_copy(slot):
        return pltpu.make_async_remote_copy(
            src_ref=sib_s.at[slot], dst_ref=sib_r.at[slot],
            send_sem=sib_ss.at[slot], recv_sem=sib_rs.at[slot],
            device_id=sibling, device_id_type=MESH,
        )

    def right_copy(slot):
        return pltpu.make_async_remote_copy(
            src_ref=z_s.at[slot], dst_ref=z_l.at[slot],
            send_sem=z_ss.at[slot], recv_sem=z_ls.at[slot],
            device_id=right, device_id_type=MESH,
        )

    def left_copy(slot):
        return pltpu.make_async_remote_copy(
            src_ref=z_s.at[slot], dst_ref=z_r.at[slot],
            send_sem=z_ss.at[slot], recv_sem=z_rs.at[slot],
            device_id=left, device_id_type=MESH,
        )

    upper = z // (levels // 2)

    def to_sibling(m):
        def one(s):
            level = upper * s + (1 - upper) * (levels - 1 - s)
            slot = m * levels + level
            sib_s[slot] = piece(m, level * 2 + 1 - core).astype(BF16)
            sib_copy(slot).start()

        loop(levels, one)

    def chip_sum(m, level):
        slot = m * levels + level
        own = piece(m, level * 2 + core)
        sib_copy(slot).wait_recv()
        tmp[...] = own + sib_r[slot].astype(F32)

    def along_line(m):
        def one(s):
            far = levels - 1 - s

            @pl.when(far > z)
            def _():
                slot = m * levels + far
                chip_sum(m, far)

                @pl.when(z > 0)
                def _():
                    right_copy(slot).wait_recv()
                    tmp[...] += z_l[slot].astype(F32)

                z_s[slot] = tmp[...].astype(BF16)
                right_copy(slot).start()

            @pl.when(s < z)
            def _():
                slot = m * levels + s
                chip_sum(m, s)

                @pl.when(z < levels - 1)
                def _():
                    left_copy(slot).wait_recv()
                    tmp[...] += z_r[slot].astype(F32)

                z_s[slot] = tmp[...].astype(BF16)
                left_copy(slot).start()

        loop(levels - 1, one)

    def finish(m, dst):
        slot = m * levels + z
        chip_sum(m, z)

        @pl.when(z > 0)
        def _():
            right_copy(slot).wait_recv()
            tmp[...] += z_l[slot].astype(F32)

        @pl.when(z < levels - 1)
        def _():
            left_copy(slot).wait_recv()
            tmp[...] += z_r[slot].astype(F32)

        dst[0] = tmp[...]

    to_sibling(0)
    loop(owners - 1, lambda k: exchange(xs, ors, o_ss, o_rs, k).start())

    def backward_tile(j):
        cols = pl.ds(pl.multiple_of(j * ft, 128), ft)
        grad = dot_nn(cr[...], wd[:, cols])
        a = pre_g[:, cols]
        s = jax.nn.sigmoid(a)
        gpg[:, cols] = (grad * pre_u[:, cols] * s * (1.0 + a * (1.0 - s))).astype(BF16)
        gpu[:, cols] = (grad * a * s).astype(BF16)

    loop(ff // ft, backward_tile)
    to_sibling(1)
    to_sibling(2)
    along_line(0)

    loop(owners - 1, lambda k: exchange(cs, cr, c_ss, c_rs, k).wait_send())

    def grad_tile(j):
        cols = pl.ds(pl.multiple_of(j * dt, 128), dt)
        cs[:, cols] = (dot_nt(gpg[...], wg[cols, :]) + dot_nt(gpu[...], wu[cols, :])).astype(BF16)

    loop(width // dt, grad_tile)
    grs[block(me)] = cs[block(me)]
    loop(owners - 1, lambda k: exchange(cs, grs, g_ss, g_rs, k).start())

    along_line(1)
    along_line(2)

    loop(owners - 1, lambda k: exchange(xs, ors, o_ss, o_rs, k).wait_recv())
    product = jnp.zeros((tok_count, 1), F32)
    for j in range(width // dt):
        cols = pl.ds(j * dt, dt)
        mixed = dot_tn(onehot[...], ors[:, cols])
        out_ref[:, cols] = (share * mixed).astype(BF16)
        product += jnp.sum(ups_ref[:, cols].astype(F32) * mixed, axis=1, keepdims=True)
    first = (lax.broadcasted_iota(jnp.int32, probs.shape, 1) == 0).astype(F32)
    gprob_ref[...] = (first - share) * (product / total)

    loop(owners - 1, lambda k: exchange(cs, grs, g_ss, g_rs, k).wait_recv())

    def unpack_tile(j):
        cols = pl.ds(pl.multiple_of(j * dt, 128), dt)
        gtok_ref[:, cols] = dot_tn(onehot[...], grs[:, cols]).astype(BF16)

    loop(width // dt, unpack_tile)

    finish(0, gdown_ref)
    finish(1, ggate_ref)
    finish(2, gup_ref)

    loop(owners - 1, lambda k: exchange(xs, ors, o_ss, o_rs, k).wait_send())
    loop(owners - 1, lambda k: exchange(cs, grs, g_ss, g_rs, k).wait_send())
    loop(3 * levels, lambda slot: sib_copy(slot).wait_send())

    def sent(slot):
        @pl.when(lax.rem(slot, levels) != z)
        def _():
            right_copy(slot).wait_send()

    loop(3 * levels, sent)


def per_device(tokens, expert_ids, gate_probs, upstream, w_gate, w_up, w_down):
    tok_count, width = tokens.shape
    owners = lax.axis_size("expert")
    copies = lax.axis_size("dp")
    ff = w_gate.shape[2]
    capacity = tok_count // owners * 5 // 2
    cap = -(-capacity // CAP_ALIGN) * CAP_ALIGN
    slots = owners * cap
    levels = copies // 2
    rows = width // copies
    vmem = pl.BlockSpec(memory_space=pltpu.VMEM)
    hbm = pl.BlockSpec(memory_space=pl.ANY)
    dma = pltpu.SemaphoreType.DMA
    weight = pltpu.VMEM((width, ff), BF16)
    wide = pltpu.VMEM((slots, width), BF16)
    narrow = pltpu.VMEM((slots, ff), BF16)
    stack = pltpu.VMEM((3 * levels, rows, ff), BF16)
    grad = jax.ShapeDtypeStruct((1, rows, ff), F32)
    return pl.pallas_call(
        functools.partial(moe_kernel, owners, copies, cap),
        out_shape=(
            jax.ShapeDtypeStruct((tok_count, width), BF16),
            jax.ShapeDtypeStruct((tok_count, width), BF16),
            jax.ShapeDtypeStruct(gate_probs.shape, F32),
            grad, grad, grad,
        ),
        in_specs=[vmem, vmem, vmem, vmem, hbm, hbm, hbm],
        out_specs=(vmem,) * 6,
        scratch_shapes=[
            weight, weight, weight,
            pltpu.VMEM((slots, tok_count), BF16),
            wide, wide, wide, wide, wide, wide,
            pltpu.VMEM((slots, ff), F32), pltpu.VMEM((slots, ff), F32),
            narrow, narrow, narrow,
            stack, stack, stack, stack, stack,
            pltpu.VMEM((rows, ff), F32),
            dma((3,)),
            *[dma((owners - 1,))] * 8,
            *[dma((3 * levels,))] * 5,
        ],
        compiler_params=pltpu.CompilerParams(
            collective_id=0, has_side_effects=True, vmem_limit_bytes=62 * 2**20
        ),
    )(expert_ids[:, 0].reshape(1, -1), gate_probs, tokens, upstream, w_gate, w_up, w_down)


CAP_ALIGN = 16


def solution(mesh):
    rows = P(("dp", "expert"), None)
    experts = P("expert", None, None)
    grads = P("expert", "dp", None)
    return jax.shard_map(
        per_device,
        mesh=mesh,
        in_specs=(rows, rows, rows, rows, experts, experts, experts),
        out_specs=(rows, rows, rows, grads, grads, grads),
        check_vma=False,
    )
```

time: 295 us -> 160 us (0.54)
  waiting for transfers between devices: 178 us -> 0 us
  Pallas kernels: 0 us -> 148 us
  matrix products: 35.9 us -> 0 us
  local copies, waits for them, and re-layouts: 36.7 us -> 11 us
  starting transfers between devices: 18.6 us -> 0 us
  between operations: 14.2 us -> 0.67 us
  other arithmetic: 10.4 us -> 0 us
    pallas_call x0 -> x1, Pallas kernels: none -> 148 us  [per_device(): pl.pallas_call(functools.partial(moe_kernel, owners, copies, cap), out_sh...]
    reduce_scatter x2 -> x0, waiting for transfers between devices: 127 us -> none  [the longest x1 68.4 us: per_device(): lax.psum_scatter(contract_rows(cot_arrived, hidden), 'dp', scatter_dimens...]
    all_to_all x4 -> x0, waiting for transfers between devices: 50.6 us -> none  [the longest x1 15.4 us: per_device(): lax.all_to_all(pack_rows(cotangent), 'expert', split_axis=0, concat_axis=...]
    dot_general x8 -> x0, matrix products: 35.9 us -> none  [the longest x2 12.6 us: contract_rows(): lax.dot_general(left, right, (((0,), (0,)), ((), ())), preferred_element_...]
    reshape x8 -> x0, local copies, waits for them, and re-layouts: 20.2 us -> none  [the longest x2 5.1 us: unpack_rows(): return blocks.reshape(owners * capacity, blocks.shape[2])[target]]
    all_to_all x4 -> x0, starting transfers between devices: 18.3 us -> none  [the longest x1 5.16 us: per_device(): lax.all_to_all(pack_rows(cotangent), 'expert', split_axis=0, concat_axis=...]
    gather x2 -> x0, local copies, waits for them, and re-layouts: 8.37 us -> none  [unpack_rows(): return blocks.reshape(owners * capacity, blocks.shape[2])[target]]
    unnamed x13 -> x12, local copies, waits for them, and re-layouts: 1.05 us -> 8.05 us
  transfers between devices with their start and end apart: 6 -> 0, of which waited for: 6 -> 0; matrix products, arithmetic and copies ran while one was open for 19% -> 0% of each run, Pallas kernels for 0% -> 0%
where the time goes in v1:
time: 160 us
  Pallas kernels  148 us (92%)
  local copies, waits for them, and re-layouts  11 us (7%)
    pallas_call x1, Pallas kernels, per_device(): pl.pallas_call(functools.partial(moe_kernel, owners, copies, cap), out_sh...  148 us
    unnamed x12, local copies, waits for them, and re-layouts  8.05 us

profile of v1, /device:TPU:0, one launch (start us, length us, event | category | flops | bytes accessed | tf_op | source)
XLA Modules:
  0.0 159.7 jit_solution(4673133941616640303)
XLA Ops:
  0.6 1.3 slice_bitcast_fusion.ids_ref
  1.9 1.4 copy.13.probs_ref
  3.3 148.1 %shard_map.118 = (bf16[160,2048]{1,0:T(8,128)(2,1)}, bf16[160,2048]{1,0:T(8,128)(2,1)}, f32[160,8]{1,0:T(8,128)}, f32[1,256,768]{2,1,0:T(8,128)}, f32[1,256,768]{2,1,0:T(8,128)}, /*index=5*/f32[1,256,768]{2,1,0:T(8,128)}) custom-call(s32[1,160]{1,0:T(1,128)} %slice_bitcast_fusion.ids_ref, f32[160,8]{1,0:T(8,128)} %copy.13.probs_ref, ...), custom_call_target="tpu_custom_call" | custom-call | tf_op jit(solution)/shard_map/pallas_call | solution.py:329
  151.4 0.0 copy-start.2
  151.4 0.0 copy-start.1
  151.4 0.0 copy-start
  151.4 1.7 %copy.14 = f32[160,8]{0,1:T(8,128)} copy(f32[160,8]{1,0:T(8,128)} %get-tuple-element.8) | data formatting | bytes 10240 | tf_op jit(solution)/shard_map/pallas_call | solution.py:329
  153.1 2.0 %copy.20 = bf16[160,2048]{1,0:T(8,128)(2,1)} copy(bf16[160,2048]{1,0:T(8,128)(2,1)} %get-tuple-element.18) | data formatting | bytes 1310720
  155.1 2.0 %copy.21 = bf16[160,2048]{1,0:T(8,128)(2,1)} copy(bf16[160,2048]{1,0:T(8,128)(2,1)} %get-tuple-element.19) | data formatting | bytes 1310720
  157.1 0.0 copy-done.2
  157.1 0.9 copy.22
  158.0 0.0 copy-done.1
  158.0 0.9 copy.23
  158.9 0.0 copy-done
  158.9 0.9 copy.24
Async XLA Ops:
  151.4 5.7 %copy-start.2 = (f32[1,256,768]{2,1,0:T(8,128)S(1)}, f32[1,256,768]{2,1,0:T(8,128)}, u32[]{:S(2)}) copy-start(f32[1,256,768]{2,1,0:T(8,128)} %get-tuple-element.21) | copy-start | bytes 2359300
  151.4 6.6 %copy-start.1 = (f32[1,256,768]{2,1,0:T(8,128)S(1)}, f32[1,256,768]{2,1,0:T(8,128)}, u32[]{:S(2)}) copy-start(f32[1,256,768]{2,1,0:T(8,128)} %get-tuple-element.22) | copy-start | bytes 2359300
  151.4 7.4 %copy-start = (f32[1,256,768]{2,1,0:T(8,128)S(1)}, f32[1,256,768]{2,1,0:T(8,128)}, u32[]{:S(2)}) copy-start(f32[1,256,768]{2,1,0:T(8,128)} %get-tuple-element.23) | copy-start | bytes 2359300

commit v2 on v1

--- a/solution.py
+++ b/solution.py
@@ -80,7 +80,7 @@
     def _():
         pl.semaphore_signal(barrier, inc=1, device_id=right, device_id_type=MESH)
 
-    ids = ids_ref[...]
+    ids = ids_ref[0:1, :]
     experts = lax.broadcasted_iota(jnp.int32, (max(owners, 8), tok_count), 0)
     match = (experts == ids).astype(BF16)
     before = (
@@ -93,8 +93,9 @@
     onehot[...] = (slots == target).astype(BF16)
 
     probs = probs_ref[...]
-    total = jnp.sum(probs, axis=1, keepdims=True)
-    share = probs[:, 0:1] / total
+    total = jnp.sum(probs, axis=0, keepdims=True)
+    share_row = probs[0:1, :] / total
+    share = jnp.transpose(jnp.broadcast_to(share_row, (8, tok_count)))[:, 0:1]
 
     def block(index):
         return pl.ds(pl.multiple_of(index * cap, 8), cap)
@@ -124,7 +125,33 @@
 
     dispatch(tok_ref, xs, xr, x_ss, x_rs)
     gtok_ref[...] = (share * ups_ref[...].astype(F32)).astype(BF16)
-    dispatch(gtok_ref, cs, cr, c_ss, c_rs)
+
+    upper = z // (levels // 2)
+    chunk = 2 * rows
+
+    def level_at(s):
+        return upper * s + (1 - upper) * (levels - 1 - s)
+
+    def cot_copy(s, k):
+        peer = lax.rem(me + k + 1, owners)
+        cols = pl.ds(pl.multiple_of(level_at(s) * chunk, 128), chunk)
+        index = s * (owners - 1) + k
+        return pltpu.make_async_remote_copy(
+            src_ref=cs.at[block(peer), cols],
+            dst_ref=cr.at[block(me), cols],
+            send_sem=c_ss.at[index],
+            recv_sem=c_rs.at[index],
+            device_id={"expert": peer},
+            device_id_type=MESH,
+        )
+
+    def send_chunk(s):
+        cols = pl.ds(pl.multiple_of(level_at(s) * chunk, 128), chunk)
+        cs[:, cols] = dot_nn(onehot[...], gtok_ref[:, cols]).astype(BF16)
+        loop(owners - 1, lambda k: cot_copy(s, k).start())
+        cr[block(me), cols] = cs[block(me), cols]
+
+    loop(levels, send_chunk)
 
     w_copies[0].wait()
     w_copies[1].wait()
@@ -140,18 +167,6 @@
 
     loop(ff // ft, forward_tile)
 
-    w_copies[2].wait()
-    loop(owners - 1, lambda k: exchange(xs, xr, x_ss, x_rs, k).wait_send())
-
-    def out_tile(j):
-        cols = pl.ds(pl.multiple_of(j * dt, 128), dt)
-        xs[:, cols] = dot_nt(hid[...], wd[cols, :]).astype(BF16)
-
-    loop(width // dt, out_tile)
-    ors[block(me)] = xs[block(me)]
-
-    loop(owners - 1, lambda k: exchange(cs, cr, c_ss, c_rs, k).wait_recv())
-
     sides = ((cr, hid), (xr, gpg), (xr, gpu))
 
     def piece(m, dest):
@@ -180,16 +195,11 @@
             device_id=left, device_id_type=MESH,
         )
 
-    upper = z // (levels // 2)
-
-    def to_sibling(m):
-        def one(s):
-            level = upper * s + (1 - upper) * (levels - 1 - s)
-            slot = m * levels + level
-            sib_s[slot] = piece(m, level * 2 + 1 - core).astype(BF16)
-            sib_copy(slot).start()
-
-        loop(levels, one)
+    def to_sibling(m, s):
+        level = level_at(s)
+        slot = m * levels + level
+        sib_s[slot] = piece(m, level * 2 + 1 - core).astype(BF16)
+        sib_copy(slot).start()
 
     def chip_sum(m, level):
         slot = m * levels + level
@@ -197,37 +207,34 @@
         sib_copy(slot).wait_recv()
         tmp[...] = own + sib_r[slot].astype(F32)
 
-    def along_line(m):
-        def one(s):
-            far = levels - 1 - s
-
-            @pl.when(far > z)
+    def along_line(m, s):
+        far = levels - 1 - s
+
+        @pl.when(far > z)
+        def _():
+            slot = m * levels + far
+            chip_sum(m, far)
+
+            @pl.when(z > 0)
             def _():
-                slot = m * levels + far
-                chip_sum(m, far)
-
-                @pl.when(z > 0)
-                def _():
-                    right_copy(slot).wait_recv()
-                    tmp[...] += z_l[slot].astype(F32)
-
-                z_s[slot] = tmp[...].astype(BF16)
-                right_copy(slot).start()
-
-            @pl.when(s < z)
+                right_copy(slot).wait_recv()
+                tmp[...] += z_l[slot].astype(F32)
+
+            z_s[slot] = tmp[...].astype(BF16)
+            right_copy(slot).start()
+
+        @pl.when(s < z)
+        def _():
+            slot = m * levels + s
+            chip_sum(m, s)
+
+            @pl.when(z < levels - 1)
             def _():
-                slot = m * levels + s
-                chip_sum(m, s)
-
-                @pl.when(z < levels - 1)
-                def _():
-                    left_copy(slot).wait_recv()
-                    tmp[...] += z_r[slot].astype(F32)
-
-                z_s[slot] = tmp[...].astype(BF16)
-                left_copy(slot).start()
-
-        loop(levels - 1, one)
+                left_copy(slot).wait_recv()
+                tmp[...] += z_r[slot].astype(F32)
+
+            z_s[slot] = tmp[...].astype(BF16)
+            left_copy(slot).start()
 
     def finish(m, dst):
         slot = m * levels + z
@@ -245,8 +252,19 @@
 
         dst[0] = tmp[...]
 
-    to_sibling(0)
-    loop(owners - 1, lambda k: exchange(xs, ors, o_ss, o_rs, k).start())
+    edge = z * (levels - 1 - z) == 0
+
+    def first_matrix(s):
+        loop(owners - 1, lambda k: cot_copy(s, k).wait_recv())
+        to_sibling(0, s)
+
+        @pl.when(jnp.logical_and(edge, s > 0))
+        def _():
+            along_line(0, s - 1)
+
+    loop(levels, first_matrix)
+
+    w_copies[2].wait()
 
     def backward_tile(j):
         cols = pl.ds(pl.multiple_of(j * ft, 128), ft)
@@ -257,11 +275,29 @@
         gpu[:, cols] = (grad * a * s).astype(BF16)
 
     loop(ff // ft, backward_tile)
-    to_sibling(1)
-    to_sibling(2)
-    along_line(0)
-
-    loop(owners - 1, lambda k: exchange(cs, cr, c_ss, c_rs, k).wait_send())
+    loop(levels, lambda s: to_sibling(1, s))
+    loop(levels, lambda s: to_sibling(2, s))
+
+    @pl.when(edge)
+    def _():
+        loop(levels - 1, lambda s: along_line(1, s))
+        loop(levels - 1, lambda s: along_line(2, s))
+
+    @pl.when(jnp.logical_not(edge))
+    def _():
+        loop(levels - 1, lambda s: along_line(0, s))
+
+    loop(owners - 1, lambda k: exchange(xs, xr, x_ss, x_rs, k).wait_send())
+
+    def out_tile(j):
+        cols = pl.ds(pl.multiple_of(j * dt, 128), dt)
+        xs[:, cols] = dot_nt(hid[...], wd[cols, :]).astype(BF16)
+
+    loop(width // dt, out_tile)
+    ors[block(me)] = xs[block(me)]
+    loop(owners - 1, lambda k: exchange(xs, ors, o_ss, o_rs, k).start())
+
+    loop(levels, lambda s: loop(owners - 1, lambda k: cot_copy(s, k).wait_send()))
 
     def grad_tile(j):
         cols = pl.ds(pl.multiple_of(j * dt, 128), dt)
@@ -271,8 +307,10 @@
     grs[block(me)] = cs[block(me)]
     loop(owners - 1, lambda k: exchange(cs, grs, g_ss, g_rs, k).start())
 
-    along_line(1)
-    along_line(2)
+    @pl.when(jnp.logical_not(edge))
+    def _():
+        loop(levels - 1, lambda s: along_line(1, s))
+        loop(levels - 1, lambda s: along_line(2, s))
 
     loop(owners - 1, lambda k: exchange(xs, ors, o_ss, o_rs, k).wait_recv())
     product = jnp.zeros((tok_count, 1), F32)
@@ -281,8 +319,9 @@
         mixed = dot_tn(onehot[...], ors[:, cols])
         out_ref[:, cols] = (share * mixed).astype(BF16)
         product += jnp.sum(ups_ref[:, cols].astype(F32) * mixed, axis=1, keepdims=True)
-    first = (lax.broadcasted_iota(jnp.int32, probs.shape, 1) == 0).astype(F32)
-    gprob_ref[...] = (first - share) * (product / total)
+    first = (lax.broadcasted_iota(jnp.int32, probs.shape, 0) == 0).astype(F32)
+    product_row = jnp.transpose(jnp.broadcast_to(product, (tok_count, 128)))[0:1, :]
+    gprob_ref[...] = (first - share_row) * (product_row / total)
 
     loop(owners - 1, lambda k: exchange(cs, grs, g_ss, g_rs, k).wait_recv())
 
@@ -326,12 +365,12 @@
     narrow = pltpu.VMEM((slots, ff), BF16)
     stack = pltpu.VMEM((3 * levels, rows, ff), BF16)
     grad = jax.ShapeDtypeStruct((1, rows, ff), F32)
-    return pl.pallas_call(
+    layer_out, grad_tokens, grad_probs, grad_gate, grad_up, grad_down = pl.pallas_call(
         functools.partial(moe_kernel, owners, copies, cap),
         out_shape=(
             jax.ShapeDtypeStruct((tok_count, width), BF16),
             jax.ShapeDtypeStruct((tok_count, width), BF16),
-            jax.ShapeDtypeStruct(gate_probs.shape, F32),
+            jax.ShapeDtypeStruct(gate_probs.shape[::-1], F32),
             grad, grad, grad,
         ),
         in_specs=[vmem, vmem, vmem, vmem, hbm, hbm, hbm],
@@ -345,13 +384,16 @@
             stack, stack, stack, stack, stack,
             pltpu.VMEM((rows, ff), F32),
             dma((3,)),
-            *[dma((owners - 1,))] * 8,
+            dma((owners - 1,)), dma((owners - 1,)),
+            dma((levels * (owners - 1),)), dma((levels * (owners - 1),)),
+            *[dma((owners - 1,))] * 4,
             *[dma((3 * levels,))] * 5,
         ],
         compiler_params=pltpu.CompilerParams(
             collective_id=0, has_side_effects=True, vmem_limit_bytes=62 * 2**20
         ),
-    )(expert_ids[:, 0].reshape(1, -1), gate_probs, tokens, upstream, w_gate, w_up, w_down)
+    )(expert_ids.T, gate_probs.T, tokens, upstream, w_gate, w_up, w_down)
+    return (layer_out, grad_tokens, grad_probs.T, grad_gate, grad_up, grad_down)
 
 
 CAP_ALIGN = 16

time: 160 us -> 140 us (0.88)
  Pallas kernels: 148 us -> 131 us
  local copies, waits for them, and re-layouts: 11 us -> 8.06 us
    pallas_call x1, Pallas kernels: 148 us -> 131 us  [per_device(): pl.pallas_call(functools.partial(moe_kernel, owners, copies, cap), out_sh...]
    pallas_call x1 -> x0, local copies, waits for them, and re-layouts: 1.7 us -> none  [per_device(): pl.pallas_call(functools.partial(moe_kernel, owners, copies, cap), out_sh...]
where the time goes in v2:
time: 140 us; the launch traced here: 139 us
  Pallas kernels  131 us (94%)
  local copies, waits for them, and re-layouts  8.06 us (6%)
    pallas_call x1, Pallas kernels, per_device(): pl.pallas_call(functools.partial(moe_kernel, owners, copies, cap), out_sh...  131 us
    unnamed x12, local copies, waits for them, and re-layouts  8.06 us

profile of v2, /device:TPU:0, one launch (start us, length us, event | category | flops | bytes accessed | tf_op | source)
XLA Modules:
  0.0 139.4 jit_solution(10066358896221847402)
XLA Ops:
  0.6 130.6 %shard_map.118 = (bf16[160,2048]{1,0:T(8,128)(2,1)}, bf16[160,2048]{1,0:T(8,128)(2,1)}, f32[8,160]{1,0:T(8,128)}, f32[1,256,768]{2,1,0:T(8,128)}, f32[1,256,768]{2,1,0:T(8,128)}, /*index=5*/f32[1,256,768]{2,1,0:T(8,128)}) custom-call(s32[8,160]{1,0:T(8,128)} %bitcast.4, f32[8,160]{1,0:T(8,128)} %bitcast.5, bf16[160,2048]{1,0:T(8,128)(2,1)} %tok_ref.1, ...), custom_call_target="tpu_custom_call" | custom-call | tf_op jit(solution)/shard_map/pallas_call | solution.py:368
  131.3 0.0 copy-start.2
  131.3 0.0 copy-start.1
  131.3 0.0 copy-start
  131.3 2.1 %copy.19 = bf16[160,2048]{1,0:T(8,128)(2,1)} copy(bf16[160,2048]{1,0:T(8,128)(2,1)} %get-tuple-element.24) | data formatting | bytes 1310720
  133.4 2.0 %copy.20 = bf16[160,2048]{1,0:T(8,128)(2,1)} copy(bf16[160,2048]{1,0:T(8,128)(2,1)} %get-tuple-element.25) | data formatting | bytes 1310720
  135.4 1.3 copy.21
  136.7 0.0 copy-done.2
  136.7 0.9 copy.22
  137.6 0.0 copy-done.1
  137.6 0.9 copy.23
  138.5 0.0 copy-done
  138.5 0.9 copy.24
Async XLA Ops:
  131.3 5.4 %copy-start.2 = (f32[1,256,768]{2,1,0:T(8,128)S(1)}, f32[1,256,768]{2,1,0:T(8,128)}, u32[]{:S(2)}) copy-start(f32[1,256,768]{2,1,0:T(8,128)} %get-tuple-element.27) | copy-start | bytes 2359300
  131.3 6.3 %copy-start.1 = (f32[1,256,768]{2,1,0:T(8,128)S(1)}, f32[1,256,768]{2,1,0:T(8,128)}, u32[]{:S(2)}) copy-start(f32[1,256,768]{2,1,0:T(8,128)} %get-tuple-element.28) | copy-start | bytes 2359300
  131.3 7.2 %copy-start = (f32[1,256,768]{2,1,0:T(8,128)S(1)}, f32[1,256,768]{2,1,0:T(8,128)}, u32[]{:S(2)}) copy-start(f32[1,256,768]{2,1,0:T(8,128)} %get-tuple-element.29) | copy-start | bytes 2359300
